TPU v7x, 256 devices: a whole 4x4x8 slice. The times are simulated.
256 devices in a mesh: dp: 64 (over z, x, y_hi), tensor: 4 (over y_lo, core).
Axes of the slice: x: 4, y: 4 (y_hi: 2, y_lo: 2; y = y_hi * 2 + y_lo), z: 8, core: 2. Of those that a mesh axis runs over, the one named last changes fastest.
Arguments:
- inputs: float32 [64, 197, 768], P('dp')
- cotangent: float32 [64, 197, 768], P('dp'), may hold values from -6 to 6
- norm_gains: float32 [2, 768], P(None, 'dp'), may hold values from 0.5 to 1.5
- attn_mats: float32 [4, 768, 768], P(None, 'dp', 'tensor')
- router: float32 [768, 3], P('dp'), may hold values from -0.4375 to 0.4375
- expert_in: float32 [3, 768, 1536], P(None, 'dp', 'tensor'), may hold values from -0.21875 to 0.21875
- expert_out: float32 [3, 768, 1536], P(None, 'dp', 'tensor'), may hold values from -0.3125 to 0.3125
- moment_gains: float32 [2, 768], P(None, 'dp'), may hold values from -128 to 128
- moment_attn: float32 [4, 768, 768], P(None, 'dp', 'tensor'), may hold values from -32 to 32
- moment_router: float32 [768, 3], P('dp'), may hold values from -320 to 320
- moment_in: float32 [3, 768, 1536], P(None, 'dp', 'tensor'), may hold values from -32 to 32
- moment_out: float32 [3, 768, 1536], P(None, 'dp', 'tensor'), may hold values from -32 to 32
- routes: int32 [64, 197, 2], P('dp'), may hold values from 0 to 2, all different within a row; in each aligned block of 197 rows (0 to 196, 197 to 393, ..., all dimensions but the last counted through in order) at most 197 rows name the same one
Outputs:
- output: float32 [64, 197, 768], P('dp')
- grad_inputs: float32 [64, 197, 768], P('dp')
- grad_gains: float32 [2, 768], P(None, 'dp')
- grad_attn: float32 [4, 768, 768], P(None, 'dp', 'tensor')
- grad_router: float32 [768, 3], P('dp')
- grad_in: float32 [3, 768, 1536], P(None, 'dp', 'tensor')
- grad_out: float32 [3, 768, 1536], P(None, 'dp', 'tensor')
- gains_new: float32 [2, 768], P(None, 'dp')
- attn_new: float32 [4, 768, 768], P(None, 'dp', 'tensor')
- router_new: float32 [768, 3], P('dp')
- in_new: float32 [3, 768, 1536], P(None, 'dp', 'tensor')
- out_new: float32 [3, 768, 1536], P(None, 'dp', 'tensor')
- moment_gains_new: float32 [2, 768], P(None, 'dp')
- moment_attn_new: float32 [4, 768, 768], P(None, 'dp', 'tensor')
- moment_router_new: float32 [768, 3], P('dp')
- moment_in_new: float32 [3, 768, 1536], P(None, 'dp', 'tensor')
- moment_out_new: float32 [3, 768, 1536], P(None, 'dp', 'tensor')
Inputs may be any that keep to these rules, and one draw needn't show every extreme that they name: `routes`: in the rows of one index of dp no expert is named by more than 197 of them, a bound that some block reaches; a row's two experts differ.
All inputs are finite; a program needn't handle non-finite values.
Results may differ from a plain program's by a relative error of at most 0.025.
The roundings to bfloat16 on the way count: a program that leaves them out, or rounds other values in their place, can miss the bound.
Values may be sent and summed in bfloat16 or wider, within the bound.
A program may use at most 128 MiB of HBM per device.

v0:
```python
import math
import jax
import jax.numpy as jnp
import numpy as np
from jax import lax
from jax.sharding import PartitionSpec as P

HEAD_DIM = 64
EF = 3
NS_ITERS = 3
CAP = 197
EPSILON = 1e-06
MOMENTUM = 0.9
MUON_RATE = 0.5
SMALL_RATE = 0.5
NEWTON_A = 3.4445
NEWTON_B = -4.775
NEWTON_C = 2.0315
ROOT_HALF = 0.7071067811865476
INV_ROOT_TAU = 0.3989422804014327


def for_sending(value):
    return jax.tree.map(lambda a: a.astype(jnp.bfloat16) if a.dtype == jnp.float32 else a, value)


def round_half(operand):
    return operand.astype(jnp.bfloat16)


def settle(operand):
    return lax.optimization_barrier(operand.astype(jnp.bfloat16))


def to_single(operand):
    return operand.astype(jnp.float32)


def contract_rows(left_mat, right_mat):
    return lax.dot_general(
        left_mat, right_mat, (((0,), (0,)), ((), ())), preferred_element_type=jnp.float32
    )


def contract_cols(left_mat, right_mat):
    return lax.dot_general(
        left_mat, right_mat, (((1,), (1,)), ((), ())), preferred_element_type=jnp.float32
    )


def fold_sources(received, source_count):
    return jnp.sum(
        received.reshape((source_count, received.shape[0] // source_count) + received.shape[1:]),
        axis=0,
    )


def norm_forward(row_data, gain_row):
    center = row_data - jnp.mean(row_data, axis=-1, keepdims=True)
    inv_std = lax.rsqrt(jnp.mean(center * center, axis=-1, keepdims=True) + EPSILON)
    normal = center * inv_std
    return (normal, inv_std, round_half(normal * gain_row))


def norm_backward(grad_result, normal, inv_std, gain_row):
    scaled = grad_result * gain_row
    grad_data = inv_std * (
        scaled
        - jnp.mean(scaled, axis=-1, keepdims=True)
        - normal * jnp.mean(scaled * normal, axis=-1, keepdims=True)
    )
    return (grad_data, jnp.sum(grad_result * normal, axis=0))


def gelu_value(pre_act):
    return 0.5 * pre_act * (1.0 + lax.erf(pre_act * ROOT_HALF))


def gelu_slope(pre_act):
    return 0.5 * (1.0 + lax.erf(pre_act * ROOT_HALF)) + pre_act * INV_ROOT_TAU * jnp.exp(
        -0.5 * pre_act * pre_act
    )


def score_table(queries, key_rows):
    return jnp.einsum("bqhd,bkhd->bhqk", queries, key_rows, preferred_element_type=jnp.float32) * (
        1.0 / math.sqrt(HEAD_DIM)
    )


def attention_forward(normed, mats_half, image_count, seq_len):
    head_count = mats_half.shape[2] // HEAD_DIM

    def project(which_mat):
        return round_half(
            jnp.dot(normed, mats_half[which_mat], preferred_element_type=jnp.float32)
        ).reshape(image_count, seq_len, head_count, HEAD_DIM)

    queries = project(0)
    key_rows = project(1)
    value_rows = project(2)
    scores = score_table(queries, key_rows)
    row_peak = jnp.max(scores, axis=-1, keepdims=True)
    log_total = row_peak + jnp.log(jnp.sum(jnp.exp(scores - row_peak), axis=-1, keepdims=True))
    prob_half = round_half(jnp.exp(scores - log_total))
    attn_rows = round_half(
        jnp.einsum("bhqk,bkhd->bqhd", prob_half, value_rows, preferred_element_type=jnp.float32)
    )
    return (
        queries,
        key_rows,
        value_rows,
        log_total,
        attn_rows.reshape(image_count * seq_len, head_count * HEAD_DIM),
    )


def attention_backward(grad_attn_rows, queries, key_rows, value_rows, log_total):
    image_count, seq_len, head_count, head_size = queries.shape
    grad_heads = grad_attn_rows.reshape(image_count, seq_len, head_count, head_size)
    prob_full = jnp.exp(score_table(queries, key_rows) - log_total)
    prob_half = round_half(prob_full)
    grad_prob = jnp.einsum(
        "bqhd,bkhd->bhqk", grad_heads, value_rows, preferred_element_type=jnp.float32
    )
    grad_values = round_half(
        jnp.einsum("bhqk,bqhd->bkhd", prob_half, grad_heads, preferred_element_type=jnp.float32)
    )
    spread = jnp.sum(prob_full * grad_prob, axis=-1, keepdims=True)
    grad_scores = round_half(prob_full * (grad_prob - spread) * (1.0 / math.sqrt(HEAD_DIM)))
    grad_queries = round_half(
        jnp.einsum("bhqk,bkhd->bqhd", grad_scores, key_rows, preferred_element_type=jnp.float32)
    )
    grad_keys = round_half(
        jnp.einsum("bhqk,bqhd->bkhd", grad_scores, queries, preferred_element_type=jnp.float32)
    )
    row_total = image_count * seq_len
    full_width = head_count * head_size
    return (
        grad_queries.reshape(row_total, full_width),
        grad_keys.reshape(row_total, full_width),
        grad_values.reshape(row_total, full_width),
    )


def orthogonalize(matrix):
    current = settle(matrix * lax.rsqrt(jnp.sum(matrix * matrix) + EPSILON))
    for iteration in range(NS_ITERS):
        gram_mat = settle(contract_rows(current, current))
        square = jnp.dot(gram_mat, gram_mat, preferred_element_type=jnp.float32)
        poly_mat = round_half(NEWTON_B * to_single(gram_mat) + NEWTON_C * square)
        current = settle(
            NEWTON_A * to_single(current)
            + jnp.dot(current, poly_mat, preferred_element_type=jnp.float32)
        )
    return current


def orthogonalize_attention(block_mat):
    rows_all, slot_width = block_mat.shape
    sub_blocks = jnp.transpose(block_mat.reshape(rows_all, 2, slot_width // 2), (1, 0, 2))
    solved = jnp.stack([orthogonalize(sub_blocks[which_mat]) for which_mat in range(2)])
    return jnp.transpose(solved, (1, 0, 2)).reshape(rows_all, slot_width)


def empty_block(block_mat):
    return jnp.zeros(block_mat.shape, jnp.bfloat16)


def shards(
    inputs,
    cotangent,
    norm_gains,
    attn_mats,
    router,
    expert_in,
    expert_out,
    moment_gains,
    moment_attn,
    moment_router,
    moment_in,
    moment_out,
    routes,
):
    image_count, seq_len, model_width = inputs.shape
    dp_count = lax.axis_size("dp")
    row_count = image_count * seq_len
    small_plane = jnp.zeros((1, norm_gains.shape[1], attn_mats.shape[2]), jnp.bfloat16)
    small_plane = small_plane.at[0, :, :2].set(round_half(norm_gains).T)
    small_plane = small_plane.at[0, :, 2 : 2 + EF].set(round_half(router))
    packed = lax.all_gather(
        jnp.concatenate([round_half(attn_mats), small_plane], axis=0), "dp", axis=1, tiled=True
    )
    attn_half = packed[:4]
    gains_half = packed[4, :, :2].T
    router_half = packed[4, :, 2 : 2 + EF]
    in_half = lax.all_gather(round_half(expert_in), "dp", axis=1, tiled=True)
    out_half = lax.all_gather(round_half(expert_out), "dp", axis=1, tiled=True)
    gain_one = to_single(gains_half[0])
    gain_two = to_single(gains_half[1])
    row_in = inputs.reshape(row_count, model_width)
    normal_one, inv_one, normed_one = norm_forward(row_in, gain_one)
    queries, key_rows, value_rows, log_total, attn_rows = attention_forward(
        normed_one, attn_half, image_count, seq_len
    )
    attn_part = contract_cols(attn_rows, attn_half[3])
    attn_full = lax.psum(attn_part.astype(jnp.bfloat16), "tensor").astype(jnp.float32)
    middle = row_in + attn_full
    normal_two, inv_two, normed_two = norm_forward(middle, gain_two)
    picked = routes.reshape(row_count, 2)
    one_hot = (picked[:, :, None] == jnp.arange(EF, dtype=jnp.int32)[None, None, :]).astype(
        jnp.float32
    )
    logits = jnp.dot(normed_two, router_half, preferred_element_type=jnp.float32)
    chosen = jnp.sum(logits[:, None, :] * one_hot, axis=2)
    gate_vals = jax.nn.sigmoid(chosen - chosen[:, ::-1])
    gate_table = jnp.sum(gate_vals[:, :, None] * one_hot, axis=1)
    grad_rows = cotangent.reshape(row_count, model_width)
    pre_act = jnp.einsum("td,edf->etf", normed_two, in_half, preferred_element_type=jnp.float32)
    hidden = round_half(gelu_value(pre_act))
    expert_rows = jnp.einsum("etf,edf->etd", hidden, out_half, preferred_element_type=jnp.float32)
    moe_part = jnp.sum(gate_table.T[:, :, None] * expert_rows, axis=0)
    moe_full = lax.psum(moe_part.astype(jnp.bfloat16), "tensor").astype(jnp.float32)
    output_rows = middle + moe_full
    grad_each = jnp.sum(grad_rows[None] * expert_rows, axis=2).T
    grad_choice_part = jnp.sum(grad_each[:, None, :] * one_hot, axis=2)
    grad_expert = round_half(gate_table.T[:, :, None] * grad_rows[None])
    grad_hidden = jnp.einsum(
        "etd,edf->etf", grad_expert, out_half, preferred_element_type=jnp.float32
    )
    grad_pre = round_half(grad_hidden * gelu_slope(pre_act))
    grad_normed_part = jnp.einsum(
        "etf,edf->td", grad_pre, in_half, preferred_element_type=jnp.float32
    )
    grad_in = jnp.einsum("td,etf->edf", normed_two, grad_pre, preferred_element_type=jnp.float32)
    grad_out = jnp.einsum("etd,etf->edf", grad_expert, hidden, preferred_element_type=jnp.float32)
    joined = lax.psum(
        jnp.concatenate([grad_normed_part, grad_choice_part], axis=1).astype(jnp.bfloat16), "tensor"
    ).astype(jnp.float32)
    grad_normed_moe, grad_choice = (joined[:, :model_width], joined[:, model_width:])
    gate_prod = gate_vals[:, 0] * gate_vals[:, 1]
    grad_first = (grad_choice[:, 0] - grad_choice[:, 1]) * gate_prod
    grad_picked = jnp.stack([grad_first, -grad_first], axis=1)
    grad_logits = round_half(jnp.sum(grad_picked[:, :, None] * one_hot, axis=1))
    grad_router = contract_rows(normed_two, grad_logits)
    grad_normed_two = grad_normed_moe + contract_cols(grad_logits, router_half)
    grad_mid_norm, grad_gain_two = norm_backward(grad_normed_two, normal_two, inv_two, gain_two)
    grad_middle = grad_rows + grad_mid_norm
    grad_mid_half = round_half(grad_middle)
    grad_attn_rows = round_half(
        jnp.dot(grad_mid_half, attn_half[3], preferred_element_type=jnp.float32)
    )
    grad_proj_out = contract_rows(grad_mid_half, attn_rows)
    grad_queries, grad_keys, grad_values = attention_backward(
        grad_attn_rows, queries, key_rows, value_rows, log_total
    )
    grad_attn = jnp.stack(
        [
            contract_rows(normed_one, grad_queries),
            contract_rows(normed_one, grad_keys),
            contract_rows(normed_one, grad_values),
            grad_proj_out,
        ]
    )
    grad_normed_one_part = (
        contract_cols(grad_queries, attn_half[0])
        + contract_cols(grad_keys, attn_half[1])
        + contract_cols(grad_values, attn_half[2])
    )
    grad_normed_one = lax.psum(grad_normed_one_part.astype(jnp.bfloat16), "tensor").astype(
        jnp.float32
    )
    grad_in_norm, grad_gain_one = norm_backward(grad_normed_one, normal_one, inv_one, gain_one)
    grad_inputs_rows = grad_middle + grad_in_norm
    gains_cols = jnp.stack([grad_gain_one, grad_gain_two], axis=1)
    small_cols = jnp.concatenate([gains_cols, grad_router], axis=1)
    got_attn, got_in, got_out, got_small = (
        lax.all_to_all(
            grad_attn.astype(jnp.bfloat16), "dp", split_axis=1, concat_axis=0, tiled=True
        ).astype(grad_attn.dtype),
        lax.all_to_all(
            grad_in.astype(jnp.bfloat16), "dp", split_axis=1, concat_axis=0, tiled=True
        ).astype(grad_in.dtype),
        lax.all_to_all(
            grad_out.astype(jnp.bfloat16), "dp", split_axis=1, concat_axis=0, tiled=True
        ).astype(grad_out.dtype),
        lax.all_to_all(
            small_cols[None].astype(jnp.bfloat16), "dp", split_axis=1, concat_axis=0, tiled=True
        ).astype(jnp.float32),
    )
    sum_attn = fold_sources(got_attn, dp_count)
    sum_in = fold_sources(got_in, dp_count)
    sum_out = fold_sources(got_out, dp_count)
    sum_small = fold_sources(got_small, dp_count)[0]
    sum_gains = sum_small[:, :2].T
    sum_router = sum_small[:, 2:]
    small_step = SMALL_RATE / math.sqrt(image_count * dp_count * seq_len)
    moment_gains_new = MOMENTUM * moment_gains + sum_gains
    moment_attn_new = MOMENTUM * moment_attn + sum_attn
    moment_router_new = MOMENTUM * moment_router + sum_router
    moment_in_new = MOMENTUM * moment_in + sum_in
    moment_out_new = MOMENTUM * moment_out + sum_out
    gains_new = norm_gains - small_step * moment_gains_new
    router_new = router - small_step * moment_router_new
    look_attn = sum_attn + MOMENTUM * moment_attn_new
    look_in = sum_in + MOMENTUM * moment_in_new
    look_out = sum_out + MOMENTUM * moment_out_new
    shard_rows = look_in.shape[1]
    slot_width = look_in.shape[2]
    blocks = 2 * EF + 2
    per_owner = -(-blocks // dp_count)
    slot_count = dp_count * per_owner
    slot_list = list(range(blocks))
    block_list = [
        slot_list.index(slot_number) if slot_number in slot_list else blocks
        for slot_number in range(slot_count)
    ]
    slot_of_block = np.array(slot_list)
    block_of_slot = np.array(block_list)
    kind_of_slot = np.where(block_of_slot < 2, 0, np.where(block_of_slot < blocks, 1, 2))
    attn_slots = jnp.transpose(
        jnp.transpose(look_attn, (1, 0, 2)).reshape(shard_rows, 2, slot_width), (1, 0, 2)
    )
    stacked = jnp.concatenate(
        [attn_slots, look_in, look_out, jnp.zeros((1, shard_rows, slot_width), jnp.float32)], axis=0
    )
    outgoing = jnp.take(stacked, jnp.asarray(block_of_slot, dtype=jnp.int32), axis=0)
    arrived = lax.all_to_all(
        for_sending(outgoing), "dp", split_axis=0, concat_axis=1, tiled=True
    ).astype(outgoing.dtype)
    own_index = lax.axis_index("dp")
    kind_table = jnp.asarray(kind_of_slot, dtype=jnp.int32)
    kind_now = kind_table[own_index * per_owner + 0]
    results = [
        lax.switch(kind_now, [orthogonalize_attention, orthogonalize, empty_block], arrived[0])
    ]
    finished = jnp.stack(results)
    returned = lax.all_to_all(
        for_sending(finished), "dp", split_axis=1, concat_axis=0, tiled=True
    ).astype(finished.dtype)
    updates = to_single(jnp.take(returned, jnp.asarray(slot_of_block, dtype=jnp.int32), axis=0))
    update_attn = jnp.transpose(
        jnp.transpose(updates[0:2], (1, 0, 2)).reshape(shard_rows, 4, slot_width // 2), (1, 0, 2)
    )
    attn_new = attn_mats - MUON_RATE * update_attn
    in_new = expert_in - MUON_RATE * updates[2 : EF + 2]
    out_new = expert_out - MUON_RATE * updates[EF + 2 : 2 * EF + 2]
    output = output_rows.reshape(image_count, seq_len, model_width)
    grad_inputs = grad_inputs_rows.reshape(image_count, seq_len, model_width)
    return (
        output,
        grad_inputs,
        sum_gains,
        sum_attn,
        sum_router,
        sum_in,
        sum_out,
        gains_new,
        attn_new,
        router_new,
        in_new,
        out_new,
        moment_gains_new,
        moment_attn_new,
        moment_router_new,
        moment_in_new,
        moment_out_new,
    )


def solution(mesh):
    return jax.shard_map(
        shards,
        mesh=mesh,
        in_specs=(
            P("dp", None, None),
            P("dp", None, None),
            P(None, "dp"),
            P(None, "dp", "tensor"),
            P("dp", None),
            P(None, "dp", "tensor"),
            P(None, "dp", "tensor"),
            P(None, "dp"),
            P(None, "dp", "tensor"),
            P("dp", None),
            P(None, "dp", "tensor"),
            P(None, "dp", "tensor"),
            P("dp", None, None),
        ),
        out_specs=(
            P("dp", None, None),
            P("dp", None, None),
            P(None, "dp"),
            P(None, "dp", "tensor"),
            P("dp", None),
            P(None, "dp", "tensor"),
            P(None, "dp", "tensor"),
            P(None, "dp"),
            P(None, "dp", "tensor"),
            P("dp", None),
            P(None, "dp", "tensor"),
            P(None, "dp", "tensor"),
            P(None, "dp"),
            P(None, "dp", "tensor"),
            P("dp", None),
            P(None, "dp", "tensor"),
            P(None, "dp", "tensor"),
        ),
        check_vma=False,
    )
```

profile of v0, /device:TPU:32, one launch (start us, length us, event | category | flops | bytes accessed | tf_op | source)
XLA Modules:
  0.0 853.9 jit_solution(13263834224516836586)
XLA Ops:
  19.4 121.1 %all-gather.4.cloned.1.call-done = bf16[5,768,192]{2,0,1:T(8,128)(2,1)} async-done(((bf16[5,12,192]{2,0,1:T(8,128)(2,1)}), bf16[5,768,192]{2,0,1:T(8,128)(2,1)}) %all-gather.4.cloned.1.call-update) | async-done | bytes 1474576 | tf_op jit(solution)/shard_map/all_gather | solution.py:191
  142.6 9.2 %fusion.173 = (bf16[1,768,192]{2,0,1:T(2,128)(2,1)}, bf16[1,768,192]{2,0,1:T(2,128)(2,1)}, bf16[1,768,192]{2,0,1:T(2,128)(2,1)S(1)}, bf16[1,768,192]{2,0,1:T(2,128)(2,1)S(1)}) fusion(bf16[5,768,192]{2,0,1:T(8,128)(2,1)} %all-gather.4.cloned.1.call-done), kind=kLoop, calls=%fused_computation.301 | loop fusion | bytes 2359296 | tf_op jit(solution)/shard_map/slice | solution.py:206
  168.9 34.6 %all-reduce.6.cloned.1.call-done = bf16[197,768]{0,1:T(8,128)(2,1)} async-done(((bf16[197,768]{0,1:T(8,128)(2,1)}), bf16[197,768]{0,1:T(8,128)(2,1)}) %all-reduce.6.cloned.1.call-update) | async-done | bytes 302608 | tf_op jit(solution)/shard_map/psum | solution.py:207
  205.4 122.8 %all-gather.6.cloned.1.call-done = bf16[3,768,384]{2,0,1:T(4,128)(2,1)} async-done(((bf16[3,12,384]{2,0,1:T(4,128)(2,1)}), bf16[3,768,384]{2,0,1:T(4,128)(2,1)}) %all-gather.6.cloned.1.call-update) | async-done | bytes 1769488 | tf_op jit(solution)/shard_map/all_gather | solution.py:197
  331.5 117.3 %all-gather.8.cloned.1.call-done = bf16[3,768,384]{2,0,1:T(4,128)(2,1)} async-done(((bf16[3,12,384]{2,0,1:T(4,128)(2,1)}), bf16[3,768,384]{2,0,1:T(4,128)(2,1)}) %all-gather.8.cloned.1.call-update) | async-done | bytes 1769488 | tf_op jit(solution)/shard_map/all_gather | solution.py:198
  448.8 4.0 multiply_reduce_fusion.2
  457.4 38.1 %all-reduce.8.cloned.1.call-done = bf16[197,770]{0,1:T(8,128)(2,1)} async-done(((bf16[197,770]{0,1:T(8,128)(2,1)}), bf16[197,770]{0,1:T(8,128)(2,1)}) %all-reduce.8.cloned.1.call-update) | async-done | bytes 303396 | tf_op jit(solution)/shard_map/psum | solution.py:237
  514.2 12.9 %all-to-all-start.1 = ((bf16[4,768,192]{2,0,1:T(4,128)(2,1)}), bf16[4,768,192]{2,0,1:T(4,128)(2,1)}, u32[]{:S(2)}, u32[]{:S(2)}) async-start(bf16[4,768,192]{2,0,1:T(4,128)(2,1)} %copy.251), calls=%async_computation.1 | async-start | bytes 3145728 | tf_op jit(solution)/shard_map/all_to_all | solution.py:278
  529.1 5.2 copy.253
  534.3 34.5 %all-to-all-done.1 = bf16[4,768,192]{2,0,1:T(4,128)(2,1)} async-done(((bf16[4,768,192]{2,0,1:T(4,128)(2,1)}), bf16[4,768,192]{2,0,1:T(4,128)(2,1)}, u32[]{:S(2)}, u32[]{:S(2)}) %all-to-all-start.1) | async-done | bytes 1179680 | tf_op jit(solution)/shard_map/all_to_all | solution.py:278
  568.8 6.8 all-to-all-start.2
  580.7 51.8 %all-to-all-done.2 = bf16[3,768,384]{2,0,1:T(4,128)(2,1)} async-done(((bf16[3,768,384]{2,0,1:T(4,128)(2,1)}), bf16[3,768,384]{2,0,1:T(4,128)(2,1)}, u32[]{:S(2)}, u32[]{:S(2)}) %all-to-all-start.2) | async-done | bytes 1769504 | tf_op jit(solution)/shard_map/all_to_all | solution.py:281
  632.4 6.5 all-to-all-start.3
  650.3 4.7 reshape.538
  657.6 38.2 %all-to-all-done.3 = bf16[3,768,384]{2,0,1:T(4,128)(2,1)} async-done(((bf16[3,768,384]{2,0,1:T(4,128)(2,1)}), bf16[3,768,384]{2,0,1:T(4,128)(2,1)}, u32[]{:S(2)}, u32[]{:S(2)}) %all-to-all-start.3) | async-done | bytes 1769504 | tf_op jit(solution)/shard_map/all_to_all | solution.py:284
  699.4 4.7 reshape.539
  709.2 6.4 all-to-all-start.4
  723.1 41.8 %all-reduce.10.cloned.1.call-done = (bf16[197,768]{0,1:T(8,128)(2,1)}, bf16[197,768]{0,1:T(8,128)(2,1)}) async-done(((bf16[197,768]{0,1:T(8,128)(2,1)}, bf16[197,768]{0,1:T(8,128)(2,1)}), (bf16[197,768]{0,1:T(8,128)(2,1)}, bf16[197,768]{0,1:T(8,128)(2,1)})) %all-reduce.10.cloned.1.call-update) | async-done | bytes 605200 | tf_op jit(solution)/shard_map/psum | solution.py:223
  768.9 12.8 %all-to-all-start = ((bf16[1,768,5]{2,0,1:T(2,128)(2,1)}), bf16[1,768,5]{2,0,1:T(2,128)(2,1)}, u32[]{:S(2)}, u32[]{:S(2)}) async-start(bf16[1,768,5]{2,0,1:T(2,128)(2,1)} %copy.249), calls=%async_computation | async-start | bytes 786432 | tf_op jit(solution)/shard_map/all_to_all | solution.py:287
  782.6 8.6 %conditional.1 = (bf16[768,384]{0,1:T(8,128)(2,1)S(1)}) conditional(s32[]{:T(128)} %bitcast.63, bf16[64,12,384]{2,1,0:T(8,128)(2,1)S(1)} %all-to-all-done.4, bf16[64,12,384]{2,1,0:T(8,128)(2,1)S(1)} %all-to-all-done.4, () %tuple.25), branch_computations={%region_28.31_spmd, %region_31.0_spmd, %region_33.34_spmd} | conditional | flops 1706655744 | bytes 14450752 | solution.py:335
  796.0 5.1 reduce.33
  803.7 12.9 %all-to-all-start.5 = ((bf16[64,2,2304]{2,1,0:T(2,128)(2,1)}), bf16[64,2,2304]{2,1,0:T(2,128)(2,1)}, u32[]{:S(2)}, u32[]{:S(2)}) async-start(bf16[64,2,2304]{2,1,0:T(2,128)(2,1)} %reshape.565), calls=%async_computation.5 | async-start | bytes 1179648 | tf_op jit(solution)/shard_map/all_to_all | solution.py:338
  822.0 14.9 %all-to-all-done.5 = bf16[64,2,2304]{2,1,0:T(2,128)(2,1)} async-done(((bf16[64,2,2304]{2,1,0:T(2,128)(2,1)}), bf16[64,2,2304]{2,1,0:T(2,128)(2,1)}, u32[]{:S(2)}, u32[]{:S(2)}) %all-to-all-start.5) | async-done | bytes 589856 | tf_op jit(solution)/shard_map/all_to_all | solution.py:338
  836.9 3.8 reshape.566
  (260 shorter events, 118.9 us)
Async XLA Ops:
  7.2 133.3 %all-gather.4.cloned.1.call-start = ((), (), s32[]{:S(2)}) async-start(), calls=%async_computation.6 | async-start | bytes 3194880 | tf_op jit(solution)/shard_map/all_gather | solution.py:191
  15.6 187.9 %all-reduce.6.cloned.1.call-start = ((), (), s32[]{:S(2)}) async-start(), calls=%async_computation.7 | async-start | bytes 786432 | tf_op jit(solution)/shard_map/psum | solution.py:207
  164.2 164.0 %all-gather.6.cloned.1.call-start = ((), (), s32[]{:S(2)}) async-start(), calls=%async_computation.8 | async-start | bytes 2396160 | tf_op jit(solution)/shard_map/all_gather | solution.py:197
  165.0 283.8 %all-gather.8.cloned.1.call-start = ((), (), s32[]{:S(2)}) async-start(), calls=%async_computation.9 | async-start | bytes 2396160 | tf_op jit(solution)/shard_map/all_gather | solution.py:198
  165.7 329.9 %all-reduce.8.cloned.1.call-start = ((), (), s32[]{:S(2)}) async-start(), calls=%async_computation.10 | async-start | bytes 794624 | tf_op jit(solution)/shard_map/psum | solution.py:237
  166.3 286.6 %copy-start.10 = (f32[1,197,768]{2,1,0:T(8,128)}, f32[1,197,768]{2,1,0:T(8,128)S(1)}, u32[]{:S(2)}) copy-start(f32[1,197,768]{2,1,0:T(8,128)S(1)} %copy.306) | copy-start | bytes 1815556
  168.9 36.3 %copy-start.41 = (s32[1,197,2]{1,2,0:T(2,128)S(1)}, s32[1,197,2]{1,2,0:T(2,128)}, u32[]{:S(2)}) copy-start(s32[1,197,2]{1,2,0:T(2,128)} %param.35) | copy-start | bytes 4732
  204.8 291.9 %copy-start.47 = (f32[197]{0:T(256)}, f32[197]{0:T(256)S(1)}, u32[]{:S(2)}) copy-start(f32[197]{0:T(256)S(1)} %add_rsqrt_fusion) | copy-start | bytes 2368
  205.4 247.5 %copy-start.48 = (f32[197,3]{0,1:T(4,128)}, f32[197,3]{0,1:T(4,128)S(1)}, u32[]{:S(2)}) copy-start(f32[197,3]{0,1:T(4,128)S(1)} %select_reduce_fusion.2) | copy-start | bytes 7096
  514.2 54.6 %all-to-all-start.1 = ((bf16[4,768,192]{2,0,1:T(4,128)(2,1)}), bf16[4,768,192]{2,0,1:T(4,128)(2,1)}, u32[]{:S(2)}, u32[]{:S(2)}) async-start(bf16[4,768,192]{2,0,1:T(4,128)(2,1)} %copy.251), calls=%async_computation.1 | async-start | bytes 3145728 | tf_op jit(solution)/shard_map/all_to_all | solution.py:278
  534.3 41.3 %copy-start.11 = (f32[1,197,768]{2,1,0:T(8,128)S(1)}, f32[1,197,768]{2,1,0:T(8,128)}, u32[]{:S(2)}) copy-start(f32[1,197,768]{2,1,0:T(8,128)} %copy-done.10) | copy-start | bytes 1815556
  534.3 41.3 %copy-start.49 = (f32[197,3]{0,1:T(4,128)S(1)}, f32[197,3]{0,1:T(4,128)}, u32[]{:S(2)}) copy-start(f32[197,3]{0,1:T(4,128)} %copy-done.48) | copy-start | bytes 7096
  568.8 63.6 %all-to-all-start.2 = ((bf16[3,768,384]{2,0,1:T(4,128)(2,1)}), bf16[3,768,384]{2,0,1:T(4,128)(2,1)}, u32[]{:S(2)}, u32[]{:S(2)}) async-start(bf16[3,768,384]{2,0,1:T(4,128)(2,1)} %copy.253), calls=%async_computation.2 | async-start | bytes 4718592 | tf_op jit(solution)/shard_map/all_to_all | solution.py:281
  580.7 58.4 %copy-start.57 = (s32[64]{0:T(128)S(1)}, s32[64]{0:T(128)}, u32[]{:S(2)}) copy-start(s32[64]{0:T(128)} %constant.199) | copy-start | bytes 772
  580.7 58.4 %copy-start.27 = (bf16[197,768]{1,0:T(8,128)(2,1)S(1)}, bf16[197,768]{1,0:T(8,128)(2,1)}, u32[]{:S(2)}) copy-start(bf16[197,768]{1,0:T(8,128)(2,1)} %get-tuple-element.173) | copy-start | bytes 907780
  632.4 63.3 %all-to-all-start.3 = ((bf16[3,768,384]{2,0,1:T(4,128)(2,1)}), bf16[3,768,384]{2,0,1:T(4,128)(2,1)}, u32[]{:S(2)}, u32[]{:S(2)}) async-start(bf16[3,768,384]{2,0,1:T(4,128)(2,1)} %copy.255), calls=%async_computation.3 | async-start | bytes 4718592 | tf_op jit(solution)/shard_map/all_to_all | solution.py:284
  657.6 49.2 %copy-start.32 = (f32[3,12,384]{2,1,0:T(8,128)}, f32[3,12,384]{2,1,0:T(8,128)S(1)}, u32[]{:S(2)}) copy-start(f32[3,12,384]{2,1,0:T(8,128)S(1)} %reduce_sum.245) | copy-start | bytes 165892
  709.2 59.7 %all-to-all-start.4 = ((bf16[64,12,384]{2,1,0:T(8,128)(2,1)}), bf16[64,12,384]{2,1,0:T(8,128)(2,1)S(1)}, u32[]{:S(2)}, u32[]{:S(2)}) async-start(bf16[64,12,384]{2,1,0:T(8,128)(2,1)} %gather_fusion), calls=%async_computation.4 | async-start | bytes 1572864 | tf_op jit(solution)/shard_map/all_to_all | solution.py:328
  715.5 49.4 %copy-start.38 = (f32[768]{0:T(1024)S(1)}, f32[768]{0:T(1024)}, u32[]{:S(2)}) copy-start(f32[768]{0:T(1024)} %get-tuple-element.181) | copy-start | bytes 9220
  715.6 49.4 %copy-start.43 = (f32[197]{0:T(256)S(1)}, f32[197]{0:T(256)}, u32[]{:S(2)}) copy-start(f32[197]{0:T(256)} %copy-done.42) | copy-start | bytes 2368
  715.6 49.4 %copy-start.45 = (f32[197]{0:T(256)S(1)}, f32[197]{0:T(256)}, u32[]{:S(2)}) copy-start(f32[197]{0:T(256)} %add_rsqrt_fusion.1) | copy-start | bytes 2368
  715.6 49.4 %all-reduce.10.cloned.1.call-start = ((), (), s32[]{:S(2)}) async-start(), calls=%async_computation.11 | async-start | bytes 1572864 | tf_op jit(solution)/shard_map/psum | solution.py:223
  768.9 34.9 %all-to-all-start = ((bf16[1,768,5]{2,0,1:T(2,128)(2,1)}), bf16[1,768,5]{2,0,1:T(2,128)(2,1)}, u32[]{:S(2)}, u32[]{:S(2)}) async-start(bf16[1,768,5]{2,0,1:T(2,128)(2,1)} %copy.249), calls=%async_computation | async-start | bytes 786432 | tf_op jit(solution)/shard_map/all_to_all | solution.py:287
  803.7 33.1 %all-to-all-start.5 = ((bf16[64,2,2304]{2,1,0:T(2,128)(2,1)}), bf16[64,2,2304]{2,1,0:T(2,128)(2,1)}, u32[]{:S(2)}, u32[]{:S(2)}) async-start(bf16[64,2,2304]{2,1,0:T(2,128)(2,1)} %reshape.565), calls=%async_computation.5 | async-start | bytes 1179648 | tf_op jit(solution)/shard_map/all_to_all | solution.py:338
  (48 other events, 294.1 us)
Sparse Core Ops, SparseCore 0:
  15.7 124.7 all-gather.3
  164.4 39.1 all-reduce.5
  208.4 119.7 all-gather.5
  332.9 115.8 all-gather.7
  456.3 39.2 all-reduce.7
  719.4 45.5 all-reduce.9
where the time goes:
time: 861 us; the launch traced here: 854 us
  waiting for transfers between devices  615 us (71%)
  local copies, waits for them, and re-layouts  75.5 us (9%)
  starting transfers between devices  59 us (7%)
  other arithmetic  45.9 us (5%)
  matrix products  33.5 us (4%)
  between operations  16.3 us (2%)
    all_gather x1, waiting for transfers between devices, shards(): in_half = lax.all_gather(round_half(expert_in), 'dp', axis=1, tiled=True)  123 us
    all_gather x1, waiting for transfers between devices, shards(): lax.all_gather(jnp.concatenate([round_half(attn_mats), small_plane], axis...  121 us
    all_gather x1, waiting for transfers between devices, shards(): out_half = lax.all_gather(round_half(expert_out), 'dp', axis=1, tiled=True)  117 us
    all_to_all x1, waiting for transfers between devices, shards(): lax.all_to_all(grad_in.astype(jnp.bfloat16), 'dp', split_axis=1, concat_a...  51.8 us
    psum x1, waiting for transfers between devices, shards(): lax.psum(moe_part.astype(jnp.bfloat16), 'tensor').astype(jnp.float32)  41.8 us
    all_to_all x1, waiting for transfers between devices, shards(): lax.all_to_all(grad_out.astype(jnp.bfloat16), 'dp', split_axis=1, concat_...  38.2 us
    psum x1, waiting for transfers between devices, shards(): lax.psum(jnp.concatenate([grad_normed_part, grad_choice_part], axis=1).as...  38.1 us
    psum x1, waiting for transfers between devices, shards(): lax.psum(attn_part.astype(jnp.bfloat16), 'tensor').astype(jnp.float32)  34.6 us
  transfers between devices with their start and end apart: 12, of which 10 were waited for; matrix products, arithmetic and copies ran while one was open for 9% of the time, Pallas kernels for 0%

commit v1 on v0

--- a/solution.py
+++ b/solution.py
@@ -195,7 +195,10 @@
     gains_half = packed[4, :, :2].T
     router_half = packed[4, :, 2 : 2 + EF]
     in_half = lax.all_gather(round_half(expert_in), "dp", axis=1, tiled=True)
-    out_half = lax.all_gather(round_half(expert_out), "dp", axis=1, tiled=True)
+    out_half = jnp.concatenate(
+        lax.all_to_all(jnp.stack([round_half(expert_out)] * lax.axis_size("dp")), "dp", 0, 0),
+        axis=1,
+    )
     gain_one = to_single(gains_half[0])
     gain_two = to_single(gains_half[1])
     row_in = inputs.reshape(row_count, model_width)

time: 861 us -> 749 us (0.87)
  waiting for transfers between devices: 615 us -> 493 us
    all_gather x1 -> x0, waiting for transfers between devices: 117 us -> none  [shards(): out_half = lax.all_gather(round_half(expert_out), 'dp', axis=1, tiled=True)]
    all_gather x1, waiting for transfers between devices: 123 us -> 101 us  [shards(): in_half = lax.all_gather(round_half(expert_in), 'dp', axis=1, tiled=True)]
    all_to_all x0 -> x1, waiting for transfers between devices: none -> 15.9 us  [shards(): lax.all_to_all(jnp.stack([round_half(expert_out)] * lax.axis_size('dp')),...]
    unnamed x134 -> x139, local copies, waits for them, and re-layouts: 23.2 us -> 20.6 us
  transfers between devices with their start and end apart: 12 -> 12, of which waited for: 10 -> 10; matrix products, arithmetic and copies ran while one was open for 9% -> 10% of each run, Pallas kernels for 0% -> 0%
where the time goes in v1:
time: 749 us; the launch traced here: 741 us
  waiting for transfers between devices  493 us (66%)
  local copies, waits for them, and re-layouts  81.6 us (11%)
  starting transfers between devices  67.3 us (9%)
  other arithmetic  44 us (6%)
  matrix products  31.4 us (4%)
  between operations  15.7 us (2%)
  loops' own time  8.62 us (1%)
    all_gather x1, waiting for transfers between devices, shards(): lax.all_gather(jnp.concatenate([round_half(attn_mats), small_plane], axis...  122 us
    all_gather x1, waiting for transfers between devices, shards(): in_half = lax.all_gather(round_half(expert_in), 'dp', axis=1, tiled=True)  101 us
    all_to_all x1, waiting for transfers between devices, shards(): lax.all_to_all(grad_in.astype(jnp.bfloat16), 'dp', split_axis=1, concat_a...  51.9 us
    psum x1, waiting for transfers between devices, shards(): lax.psum(moe_part.astype(jnp.bfloat16), 'tensor').astype(jnp.float32)  41.9 us
    all_to_all x1, waiting for transfers between devices, shards(): lax.all_to_all(grad_out.astype(jnp.bfloat16), 'dp', split_axis=1, concat_...  38.1 us
    psum x1, waiting for transfers between devices, shards(): lax.psum(jnp.concatenate([grad_normed_part, grad_choice_part], axis=1).as...  38.1 us
    all_to_all x1, waiting for transfers between devices, shards(): lax.all_to_all(grad_attn.astype(jnp.bfloat16), 'dp', split_axis=1, concat...  34.5 us
    psum x1, waiting for transfers between devices, shards(): lax.psum(attn_part.astype(jnp.bfloat16), 'tensor').astype(jnp.float32)  33.9 us
  transfers between devices with their start and end apart: 12, of which 10 were waited for; matrix products, arithmetic and copies ran while one was open for 10% of the time, Pallas kernels for 0%

profile of v1, /device:TPU:32, one launch (start us, length us, event | category | flops | bytes accessed | tf_op | source)
XLA Modules:
  0.0 741.4 jit_solution(4374202172980977082)
XLA Ops:
  18.2 122.3 %all-gather.3.cloned.1.call-done = bf16[5,768,192]{2,0,1:T(8,128)(2,1)} async-done(((bf16[5,12,192]{2,0,1:T(8,128)(2,1)}), bf16[5,768,192]{2,0,1:T(8,128)(2,1)}) %all-gather.3.cloned.1.call-update) | async-done | bytes 1474576 | tf_op jit(solution)/shard_map/all_gather | solution.py:191
  143.7 9.1 %fusion.170 = (bf16[1,768,192]{2,0,1:T(2,128)(2,1)S(1)}, bf16[1,768,192]{2,0,1:T(2,128)(2,1)S(1)}, bf16[1,768,192]{2,0,1:T(2,128)(2,1)S(1)}, bf16[1,768,192]{2,0,1:T(2,128)(2,1)}) fusion(bf16[5,768,192]{2,0,1:T(8,128)(2,1)} %all-gather.3.cloned.1.call-done), kind=kLoop, calls=%fused_computation.297 | loop fusion | bytes 2359296 | tf_op jit(solution)/shard_map/slice | solution.py:209
  164.6 8.5 %all-to-all-start = ((bf16[64,3,12,384]{3,2,1,0:T(8,128)(2,1)}), bf16[64,3,12,384]{3,2,1,0:T(8,128)(2,1)}, u32[]{:S(2)}, u32[]{:S(2)}) async-start(bf16[64,3,12,384]{3,2,1,0:T(8,128)(2,1)} %stack.27), calls=%async_computation | async-start | bytes 4718592 | tf_op jit(solution)/shard_map/all_to_all | solution.py:199
  176.7 33.9 %all-reduce.6.cloned.1.call-done = bf16[197,768]{0,1:T(8,128)(2,1)} async-done(((bf16[197,768]{0,1:T(8,128)(2,1)}), bf16[197,768]{0,1:T(8,128)(2,1)}) %all-reduce.6.cloned.1.call-update) | async-done | bytes 302608 | tf_op jit(solution)/shard_map/psum | solution.py:210
  212.4 15.9 %all-to-all-done = bf16[64,3,12,384]{3,2,1,0:T(8,128)(2,1)} async-done(((bf16[64,3,12,384]{3,2,1,0:T(8,128)(2,1)}), bf16[64,3,12,384]{3,2,1,0:T(8,128)(2,1)}, u32[]{:S(2)}, u32[]{:S(2)}) %all-to-all-start) | async-done | bytes 1769504 | tf_op jit(solution)/shard_map/all_to_all | solution.py:199
  231.6 3.9 reshape.535
  235.5 101.3 %all-gather.5.cloned.1.call-done = bf16[3,768,384]{2,0,1:T(4,128)(2,1)} async-done(((bf16[3,12,384]{2,0,1:T(4,128)(2,1)}), bf16[3,768,384]{2,0,1:T(4,128)(2,1)}) %all-gather.5.cloned.1.call-update) | async-done | bytes 1769488 | tf_op jit(solution)/shard_map/all_gather | solution.py:197
  345.7 38.1 %all-reduce.8.cloned.1.call-done = bf16[197,770]{0,1:T(8,128)(2,1)} async-done(((bf16[197,770]{0,1:T(8,128)(2,1)}), bf16[197,770]{0,1:T(8,128)(2,1)}) %all-reduce.8.cloned.1.call-update) | async-done | bytes 303396 | tf_op jit(solution)/shard_map/psum | solution.py:240
  402.0 12.9 %all-to-all-start.2 = ((bf16[4,768,192]{2,0,1:T(4,128)(2,1)}), bf16[4,768,192]{2,0,1:T(4,128)(2,1)}, u32[]{:S(2)}, u32[]{:S(2)}) async-start(bf16[4,768,192]{2,0,1:T(4,128)(2,1)} %copy.241), calls=%async_computation.2 | async-start | bytes 3145728 | tf_op jit(solution)/shard_map/all_to_all | solution.py:281
  416.9 5.2 copy.243
  422.1 34.5 %all-to-all-done.2 = bf16[4,768,192]{2,0,1:T(4,128)(2,1)} async-done(((bf16[4,768,192]{2,0,1:T(4,128)(2,1)}), bf16[4,768,192]{2,0,1:T(4,128)(2,1)}, u32[]{:S(2)}, u32[]{:S(2)}) %all-to-all-start.2) | async-done | bytes 1179680 | tf_op jit(solution)/shard_map/all_to_all | solution.py:281
  456.6 6.8 all-to-all-start.3
  468.3 51.9 %all-to-all-done.3 = bf16[3,768,384]{2,0,1:T(4,128)(2,1)} async-done(((bf16[3,768,384]{2,0,1:T(4,128)(2,1)}), bf16[3,768,384]{2,0,1:T(4,128)(2,1)}, u32[]{:S(2)}, u32[]{:S(2)}) %all-to-all-start.3) | async-done | bytes 1769504 | tf_op jit(solution)/shard_map/all_to_all | solution.py:284
  520.2 6.5 all-to-all-start.4
  538.1 4.7 reshape.548
  545.4 38.1 %all-to-all-done.4 = bf16[3,768,384]{2,0,1:T(4,128)(2,1)} async-done(((bf16[3,768,384]{2,0,1:T(4,128)(2,1)}), bf16[3,768,384]{2,0,1:T(4,128)(2,1)}, u32[]{:S(2)}, u32[]{:S(2)}) %all-to-all-start.4) | async-done | bytes 1769504 | tf_op jit(solution)/shard_map/all_to_all | solution.py:287
  587.2 4.7 reshape.549
  597.0 6.5 all-to-all-start.5
  611.1 41.9 %all-reduce.10.cloned.1.call-done = (bf16[197,768]{0,1:T(8,128)(2,1)}, bf16[197,768]{0,1:T(8,128)(2,1)}) async-done(((bf16[197,768]{0,1:T(8,128)(2,1)}, bf16[197,768]{0,1:T(8,128)(2,1)}), (bf16[197,768]{0,1:T(8,128)(2,1)}, bf16[197,768]{0,1:T(8,128)(2,1)})) %all-reduce.10.cloned.1.call-update) | async-done | bytes 605200 | tf_op jit(solution)/shard_map/psum | solution.py:226
  656.8 12.8 %all-to-all-start.1 = ((bf16[1,768,5]{2,0,1:T(2,128)(2,1)}), bf16[1,768,5]{2,0,1:T(2,128)(2,1)}, u32[]{:S(2)}, u32[]{:S(2)}) async-start(bf16[1,768,5]{2,0,1:T(2,128)(2,1)} %copy.239), calls=%async_computation.1 | async-start | bytes 786432 | tf_op jit(solution)/shard_map/all_to_all | solution.py:290
  670.6 8.7 %conditional.1 = (bf16[768,384]{0,1:T(8,128)(2,1)S(1)}) conditional(s32[]{:T(128)} %bitcast.64, bf16[64,12,384]{2,1,0:T(8,128)(2,1)S(1)} %all-to-all-done.5, bf16[64,12,384]{2,1,0:T(8,128)(2,1)S(1)} %all-to-all-done.5, () %tuple.25), branch_computations={%region_28.31_spmd, %region_31.0_spmd, %region_33.34_spmd} | conditional | flops 1706655744 | bytes 14450752 | solution.py:338
  684.1 5.1 reduce.33
  691.8 12.9 %all-to-all-start.6 = ((bf16[64,2,2304]{2,1,0:T(2,128)(2,1)}), bf16[64,2,2304]{2,1,0:T(2,128)(2,1)}, u32[]{:S(2)}, u32[]{:S(2)}) async-start(bf16[64,2,2304]{2,1,0:T(2,128)(2,1)} %reshape.575), calls=%async_computation.6 | async-start | bytes 1179648 | tf_op jit(solution)/shard_map/all_to_all | solution.py:341
  710.1 14.9 %all-to-all-done.6 = bf16[64,2,2304]{2,1,0:T(2,128)(2,1)} async-done(((bf16[64,2,2304]{2,1,0:T(2,128)(2,1)}), bf16[64,2,2304]{2,1,0:T(2,128)(2,1)}, u32[]{:S(2)}, u32[]{:S(2)}) %all-to-all-start.6) | async-done | bytes 589856 | tf_op jit(solution)/shard_map/all_to_all | solution.py:341
  (268 shorter events, 124.7 us)
Async XLA Ops:
  7.2 133.3 %all-gather.3.cloned.1.call-start = ((), (), s32[]{:S(2)}) async-start(), calls=%async_computation.7 | async-start | bytes 3194880 | tf_op jit(solution)/shard_map/all_gather | solution.py:191
  15.6 194.9 %all-reduce.6.cloned.1.call-start = ((), (), s32[]{:S(2)}) async-start(), calls=%async_computation.8 | async-start | bytes 786432 | tf_op jit(solution)/shard_map/psum | solution.py:210
  18.1 634.9 %copy-start.43 = (f32[197]{0:T(256)}, f32[197]{0:T(256)S(1)}, u32[]{:S(2)}) copy-start(f32[197]{0:T(256)S(1)} %broadcast_multiply_fusion.5) | copy-start | bytes 2368
  18.2 134.6 %copy-start.48 = (f32[197]{0:T(256)}, f32[197]{0:T(256)S(1)}, u32[]{:S(2)}) copy-start(f32[197]{0:T(256)S(1)} %add_rsqrt_fusion.1) | copy-start | bytes 2368
  164.6 63.7 %all-to-all-start = ((bf16[64,3,12,384]{3,2,1,0:T(8,128)(2,1)}), bf16[64,3,12,384]{3,2,1,0:T(8,128)(2,1)}, u32[]{:S(2)}, u32[]{:S(2)}) async-start(bf16[64,3,12,384]{3,2,1,0:T(8,128)(2,1)} %stack.27), calls=%async_computation | async-start | bytes 4718592 | tf_op jit(solution)/shard_map/all_to_all | solution.py:199
  173.1 163.7 %all-gather.5.cloned.1.call-start = ((), (), s32[]{:S(2)}) async-start(), calls=%async_computation.9 | async-start | bytes 2396160 | tf_op jit(solution)/shard_map/all_gather | solution.py:197
  173.8 210.0 %all-reduce.8.cloned.1.call-start = ((), (), s32[]{:S(2)}) async-start(), calls=%async_computation.10 | async-start | bytes 794624 | tf_op jit(solution)/shard_map/psum | solution.py:240
  174.1 167.0 %copy-start.7 = (f32[1,197,768]{2,1,0:T(8,128)}, f32[1,197,768]{2,1,0:T(8,128)S(1)}, u32[]{:S(2)}) copy-start(f32[1,197,768]{2,1,0:T(8,128)S(1)} %copy.290) | copy-start | bytes 1815556
  211.7 173.3 %copy-start.45 = (f32[197]{0:T(256)}, f32[197]{0:T(256)S(1)}, u32[]{:S(2)}) copy-start(f32[197]{0:T(256)S(1)} %broadcast_multiply_fusion.4) | copy-start | bytes 2368
  211.9 173.1 %copy-start.51 = (f32[197]{0:T(256)}, f32[197]{0:T(256)S(1)}, u32[]{:S(2)}) copy-start(f32[197]{0:T(256)S(1)} %add_rsqrt_fusion) | copy-start | bytes 2368
  212.4 128.7 %copy-start.52 = (f32[197,3]{0,1:T(4,128)}, f32[197,3]{0,1:T(4,128)S(1)}, u32[]{:S(2)}) copy-start(f32[197,3]{0,1:T(4,128)S(1)} %select_reduce_fusion.2) | copy-start | bytes 7096
  402.0 54.6 %all-to-all-start.2 = ((bf16[4,768,192]{2,0,1:T(4,128)(2,1)}), bf16[4,768,192]{2,0,1:T(4,128)(2,1)}, u32[]{:S(2)}, u32[]{:S(2)}) async-start(bf16[4,768,192]{2,0,1:T(4,128)(2,1)} %copy.241), calls=%async_computation.2 | async-start | bytes 3145728 | tf_op jit(solution)/shard_map/all_to_all | solution.py:281
  422.1 41.3 %copy-start.8 = (f32[1,197,768]{2,1,0:T(8,128)S(1)}, f32[1,197,768]{2,1,0:T(8,128)}, u32[]{:S(2)}) copy-start(f32[1,197,768]{2,1,0:T(8,128)} %copy-done.7) | copy-start | bytes 1815556
  422.1 41.3 %copy-start.53 = (f32[197,3]{0,1:T(4,128)S(1)}, f32[197,3]{0,1:T(4,128)}, u32[]{:S(2)}) copy-start(f32[197,3]{0,1:T(4,128)} %copy-done.52) | copy-start | bytes 7096
  456.6 63.7 %all-to-all-start.3 = ((bf16[3,768,384]{2,0,1:T(4,128)(2,1)}), bf16[3,768,384]{2,0,1:T(4,128)(2,1)}, u32[]{:S(2)}, u32[]{:S(2)}) async-start(bf16[3,768,384]{2,0,1:T(4,128)(2,1)} %copy.243), calls=%async_computation.3 | async-start | bytes 4718592 | tf_op jit(solution)/shard_map/all_to_all | solution.py:284
  468.3 58.5 %copy-start.61 = (s32[64]{0:T(128)S(1)}, s32[64]{0:T(128)}, u32[]{:S(2)}) copy-start(s32[64]{0:T(128)} %constant.199) | copy-start | bytes 772
  468.3 58.5 %copy-start.30 = (bf16[197,768]{1,0:T(8,128)(2,1)S(1)}, bf16[197,768]{1,0:T(8,128)(2,1)}, u32[]{:S(2)}) copy-start(bf16[197,768]{1,0:T(8,128)(2,1)} %get-tuple-element.173) | copy-start | bytes 907780
  520.2 63.3 %all-to-all-start.4 = ((bf16[3,768,384]{2,0,1:T(4,128)(2,1)}), bf16[3,768,384]{2,0,1:T(4,128)(2,1)}, u32[]{:S(2)}, u32[]{:S(2)}) async-start(bf16[3,768,384]{2,0,1:T(4,128)(2,1)} %copy.245), calls=%async_computation.4 | async-start | bytes 4718592 | tf_op jit(solution)/shard_map/all_to_all | solution.py:287
  545.4 49.2 %copy-start.35 = (f32[3,12,384]{2,1,0:T(8,128)}, f32[3,12,384]{2,1,0:T(8,128)S(1)}, u32[]{:S(2)}) copy-start(f32[3,12,384]{2,1,0:T(8,128)S(1)} %reduce_sum.245) | copy-start | bytes 165892
  597.0 59.8 %all-to-all-start.5 = ((bf16[64,12,384]{2,1,0:T(8,128)(2,1)}), bf16[64,12,384]{2,1,0:T(8,128)(2,1)S(1)}, u32[]{:S(2)}, u32[]{:S(2)}) async-start(bf16[64,12,384]{2,1,0:T(8,128)(2,1)} %gather_fusion), calls=%async_computation.5 | async-start | bytes 1572864 | tf_op jit(solution)/shard_map/all_to_all | solution.py:331
  603.5 49.4 %copy-start.49 = (f32[197]{0:T(256)S(1)}, f32[197]{0:T(256)}, u32[]{:S(2)}) copy-start(f32[197]{0:T(256)} %copy-done.48) | copy-start | bytes 2368
  603.5 49.4 %all-reduce.10.cloned.1.call-start = ((), (), s32[]{:S(2)}) async-start(), calls=%async_computation.11 | async-start | bytes 1572864 | tf_op jit(solution)/shard_map/psum | solution.py:226
  656.8 35.0 %all-to-all-start.1 = ((bf16[1,768,5]{2,0,1:T(2,128)(2,1)}), bf16[1,768,5]{2,0,1:T(2,128)(2,1)}, u32[]{:S(2)}, u32[]{:S(2)}) async-start(bf16[1,768,5]{2,0,1:T(2,128)(2,1)} %copy.239), calls=%async_computation.1 | async-start | bytes 786432 | tf_op jit(solution)/shard_map/all_to_all | solution.py:290
  691.8 33.1 %all-to-all-start.6 = ((bf16[64,2,2304]{2,1,0:T(2,128)(2,1)}), bf16[64,2,2304]{2,1,0:T(2,128)(2,1)}, u32[]{:S(2)}, u32[]{:S(2)}) async-start(bf16[64,2,2304]{2,1,0:T(2,128)(2,1)} %reshape.575), calls=%async_computation.6 | async-start | bytes 1179648 | tf_op jit(solution)/shard_map/all_to_all | solution.py:341
  (51 other events, 310.6 us)
Sparse Core Ops, SparseCore 0:
  15.7 124.7 all-gather.2
  163.0 47.4 all-reduce.5
  215.4 121.3 all-gather.4
  344.5 39.2 all-reduce.7
  607.3 45.5 all-reduce.9
